TPU v7x, 32 devices: a whole 2x2x4 slice. The times are simulated.
32 devices in a mesh: row: 4 (over x, core), col: 2 (over y), layer: 4 (over z).
Axes of the slice: x: 2, y: 2, z: 4, core: 2. Of those that a mesh axis runs over, the one named last changes fastest.
Arguments:
- density_matrix: bfloat16 [2048, 2048], P('row', 'col'), may hold values from -3 to 3
- block_mask: int32 [32, 32], P('row', 'col'), may hold values 0 or 1
- intersection_weights: float32 [2048], P(('col', 'layer')), may hold values from -0.125 to 0.125
- exponents: float32 [2048], P('row'), may hold values from 0.5 to 8
- anchor_x: int32 [32], P('row'), may hold values from 0 to 31
- anchor_y: int32 [32], P('row'), may hold values from 0 to 127, as said below
- anchor_z: int32 [32], P('row'), may hold values from 0 to 127
Outputs:
- squared: bfloat16 [2048, 2048], P('row', ('col', 'layer'))
- density: float32 [128, 128, 128], P('row', ('col', 'layer'))
Inputs may be any that keep to these rules, and one draw needn't show every extreme that they name: `anchor_y`: block row a starts in the second dimension between (a mod (8)) * 16 and that plus 16 - 1.
All inputs are finite; a program needn't handle non-finite values. No bound on the sum of `block_mask` on one device may be relied on, other than what follows from the above.
Results may differ from a plain program's by a relative error of at most 0.0055.
Values may be sent and summed in bfloat16 or wider, within the bound.
A program may use at most 64 MiB of HBM per device.

v0:
```python
import functools

import jax
import jax.numpy as jnp
from jax import lax
from jax.experimental import pallas as pl
from jax.experimental.pallas import tpu as pltpu
from jax.sharding import PartitionSpec as P

BLOCK = 64
TILE = 16
SX = 32
SY = 16
GZ = 128
STEP_SQ = 0.0625
MESH = pl.DeviceIdType.MESH
F32 = jnp.float32
BF16 = jnp.bfloat16
LANES = 128
OUT_CHUNKS = 2
LOADS = 2


def dot_nt(a, b):
    return lax.dot_general(a, b, (((1,), (1,)), ((), ())), preferred_element_type=F32)


def hi_lo(x):
    high = x.astype(BF16).astype(F32)
    return jnp.concatenate([high, x - high], axis=0).astype(BF16)


def kernel(
    sizes,
    a_hbm, mask_hbm, w_hbm, e_hbm, ax_hbm, ay_hbm, az_hbm,
    sq_ref, den_ref,
    a_ref, mask_ref, w_ref, e_ref, ax_ref, ay_ref, az_ref, load_sem,
    m_buf, right, own_part, part_out, part_in, w_all, v_out, v_all, q_out, q_all, pack, pack_in, shape_xy, shape_low, shape_z,
    piece_send, piece_recv, fwd_send, part_send, part_recv,
    w_send, w_recv, v_send, v_recv, q_send, q_recv, pack_send, pack_recv,
):
    nr, nc, nl = sizes
    ratio = nr // nc
    rows, cols = a_ref.shape
    width = cols // nl
    atoms = rows // BLOCK
    r, c, l = lax.axis_index("row"), lax.axis_index("col"), lax.axis_index("layer")
    sibling = r + 1 - 2 * (r % 2)
    following = (r + 1) % nr

    def remote(src, dst, send, recv, device):
        return pltpu.make_async_remote_copy(
            src_ref=src, dst_ref=dst, send_sem=send, recv_sem=recv,
            device_id=device, device_id_type=MESH,
        )

    chunks = width // LANES
    tall = rows // LOADS
    small = [
        pltpu.make_async_copy(src, dst, load_sem.at[at])
        for at, (src, dst) in enumerate((
            (mask_hbm, mask_ref), (w_hbm, w_ref), (e_hbm, e_ref),
            (ax_hbm, ax_ref), (ay_hbm, ay_ref), (az_hbm, az_ref),
        ))
    ]
    large = [
        pltpu.make_async_copy(
            a_hbm.at[pl.ds(p * tall, tall), :], a_ref.at[pl.ds(p * tall, tall), :], load_sem.at[6 + p]
        )
        for p in range(LOADS)
    ]
    for copy in small + large:
        copy.start()

    barrier = pltpu.get_barrier_semaphore()
    peers = 0
    for dr in range(nr):
        for dc in range(nc):
            if dr or dc:
                peers += 1
                pl.semaphore_signal(
                    barrier, inc=1, device_id=((r + dr) % nr, (c + dc) % nc, l), device_id_type=MESH
                )
    for k in range(1, nl):
        peers += 1
        pl.semaphore_signal(barrier, inc=1, device_id=(r, c, (l + k) % nl), device_id_type=MESH)

    for copy in small:
        copy.wait()
    kept = jnp.where(mask_ref[...] > 0, 1.0, 0.0).astype(F32)
    spread = lax.broadcasted_iota(jnp.int32, (cols // BLOCK, cols), 1) // BLOCK
    pick = lax.broadcasted_iota(jnp.int32, (cols // BLOCK, cols), 0)
    wide = jnp.dot(kept, jnp.where(spread == pick, 1.0, 0.0).astype(F32), preferred_element_type=F32)
    w_all[l] = jnp.broadcast_to(w_ref[...], (8, width))
    lane_atom = lax.broadcasted_iota(jnp.int32, (8, rows), 1) // BLOCK
    sub = lax.broadcasted_iota(jnp.int32, (8, rows), 0)
    table = jnp.broadcast_to(e_ref[...], (8, rows))
    for j in range(atoms):
        here = lane_atom == j
        for at, ref in ((1, ax_ref), (2, ay_ref), (3, az_ref)):
            table = jnp.where(here & (sub == at), ref[j].astype(F32), table)
    pack[...] = table
    for b in range(atoms):
        if b % (atoms // LOADS) == 0:
            large[b // (atoms // LOADS)].wait()
        at = pl.ds(b * BLOCK, BLOCK)
        m_buf[at, :] = a_ref[at, :] * jnp.broadcast_to(wide[b : b + 1, :], (BLOCK, cols)).astype(BF16)

    pl.semaphore_wait(barrier, peers)

    w_copies = [
        remote(w_all.at[l], w_all.at[l], w_send.at[k - 1], w_recv.at[k - 1], (r, c, (l + k) % nl))
        for k in range(1, nl)
    ]
    for copy in w_copies:
        copy.start()
    pack_copy = remote(pack, pack_in, pack_send.at[0], pack_recv.at[0], (following, c, l))
    pack_copy.start()

    home = r // ratio
    slot = r % ratio

    def strip(h):
        return m_buf.at[:, pl.ds(pl.multiple_of(l * width + h * LANES, LANES), LANES)]

    def piece(i, cc, h):
        return right.at[i, cc, h]

    def sem_at(i, cc, h):
        return (i * nc + cc) * chunks + h

    def piece_copy(k, h):
        return remote(
            strip(h), piece(slot, c, h), piece_send.at[k * chunks + h],
            piece_recv.at[sem_at(slot, c, h)], ((r + 2 * k) % nr, home, l),
        )

    def own_copy(h):
        return pltpu.make_async_copy(strip(h), piece(slot, c, h), piece_recv.at[sem_at(slot, c, h)])

    at_home = home == c
    for h in range(chunks):
        for k in range(1, nr // 2):
            piece_copy(k, h).start()

        @pl.when(at_home)
        def _():
            own_copy(h).start()

        @pl.when(jnp.logical_not(at_home))
        def _():
            piece_copy(0, h).start()

    y_first = (c * nl + l) * SY
    y_count = nc * nl * SY

    def profiles(g, ref):
        rate = ref[0:1, :] * (-STEP_SQ)

        def profile(t):
            value = jnp.exp(rate * (t - 7.5) * (t - 7.5))
            return jnp.where((t >= 0.0) & (t < float(TILE)), value, 0.0)

        tx = lax.broadcasted_iota(jnp.int32, (SX, rows), 0).astype(F32) + float(g * SX) - ref[1:2, :]
        ty = (lax.broadcasted_iota(jnp.int32, (SY, rows), 0) + y_first).astype(F32) - ref[2:3, :]
        ty = jnp.where(ty < 0.0, ty + float(y_count), ty)
        tz = lax.broadcasted_iota(jnp.int32, (GZ, rows), 0).astype(F32) - ref[3:4, :]
        tz = jnp.where(tz < 0.0, tz + float(GZ), tz)
        px, py = profile(tx), profile(ty)
        for x in range(SX):
            plane = px[x : x + 1, :] * py
            high = plane.astype(BF16)
            shape_xy[g, x * SY : (x + 1) * SY, :] = high
            shape_low[g, x * SY : (x + 1) * SY, :] = (plane - high.astype(F32)).astype(BF16)
        shape_z[g] = profile(tz)

    profiles(0, pack)

    for copy in w_copies:
        copy.wait_recv()
    total = jnp.zeros((16, rows), F32)
    for k in range(nl):
        total = total + dot_nt(hi_lo(w_all[k]), m_buf[:, k * width : (k + 1) * width])
    v_out[...] = total[:8] + total[8:]

    def v_copy(k):
        return remote(
            v_out, v_all.at[slot, c], v_send.at[k], v_recv.at[slot * nc + c], ((r + k) % nr, home, l)
        )

    @pl.when(at_home)
    def _():
        v_all[slot, c] = v_out[...]

    @pl.when(jnp.logical_not(at_home))
    def _():
        v_copy(0).start()

    for k in range(1, nr):
        v_copy(k).start()

    pack_copy.wait_recv()
    profiles(1, pack_in)

    def direct(i):
        return (c * ratio + i) % 2 == r % 2

    def fwd_copy(i, cc, h):
        return remote(
            piece(i, cc, h), piece(i, cc, h), fwd_send.at[sem_at(i, cc, h)],
            piece_recv.at[sem_at(i, cc, h)], (sibling, c, l),
        )

    def landed(i, cc, h):
        fwd_copy(i, cc, h).wait_recv()

    def pass_on(h):
        for k in range(nc):
            cc = (c + 1 + k) % nc
            for i in range(ratio):

                @pl.when(direct(i))
                def _():
                    mine = (c * ratio + i == r) & (cc == c)

                    @pl.when(mine)
                    def _():
                        own_copy(h).wait()

                    @pl.when(jnp.logical_not(mine))
                    def _():
                        landed(i, cc, h)

                    fwd_copy(i, cc, h).start()

    def take(cc, h):
        for i in range(ratio):

            @pl.when(jnp.logical_not(direct(i)))
            def _():
                landed(i, cc, h)

    low = rows // OUT_CHUNKS

    def product(cc, h, at):
        total = jnp.dot(m_buf[at, 0:rows], right[0, cc, h], preferred_element_type=F32)
        for i in range(1, ratio):
            total = total + jnp.dot(
                m_buf[at, i * rows : (i + 1) * rows], right[i, cc, h], preferred_element_type=F32
            )
        return total

    def part_copy(k, h, o):
        at = pl.ds(o * low, low)
        index = ((k - 1) * chunks + h) * OUT_CHUNKS + o
        return remote(
            part_out.at[k - 1, h, at, :], part_in.at[k - 1, h, at, :], part_send.at[index],
            part_recv.at[index], (r, (c + k) % nc, l),
        )

    def parts(h):
        for k in range(1, nc):
            take((c + k) % nc, h)
            for o in range(OUT_CHUNKS):
                at = pl.ds(o * low, low)
                part_out[k - 1, h, at, :] = product((c + k) % nc, h, at).astype(BF16)
                part_copy(k, h, o).start()

    def charge_share():
        for i in range(ratio):
            for cc in range(nc):

                @pl.when(jnp.logical_not((c * ratio + i == r) & (cc == c)))
                def _():
                    remote(
                        v_out, v_all.at[i, cc], v_send.at[0], v_recv.at[i * nc + cc], (r, c, l)
                    ).wait_recv()

        total = jnp.zeros((16, rows), F32)
        for i in range(ratio):
            v = v_all[i, 0]
            for cc in range(1, nc):
                v = v + v_all[i, cc]
            total = total + dot_nt(hi_lo(v), m_buf[:, i * rows : (i + 1) * rows])
        q_out[...] = total[:8] + total[8:]
        q_all[0, c] = q_out[...]

    def q_copy(g, k):
        return remote(
            q_out, q_all.at[g, c], q_send.at[g * nc + k], q_recv.at[g * nc + k],
            ((r + g) % nr, (c + k) % nc, l),
        )

    sent_q = [(g, k) for g in range(2) for k in range(nc) if g or k]
    for h in range(chunks):
        pass_on(h)
        if h == chunks - 1:
            charge_share()
            for g, k in sent_q:
                q_copy(g, k).start()
        parts(h)

    for h in range(chunks):
        take(c, h)
        for o in range(OUT_CHUNKS):
            at = pl.ds(o * low, low)
            own_part[h, at, :] = product(c, h, at)

    for g, k in sent_q:
        q_copy(g, k).wait_recv()
    total = jnp.zeros((SX * SY, GZ), F32)
    for g in range(2):
        charge = q_all[g, 0]
        for cc in range(1, nc):
            charge = charge + q_all[g, cc]
        value = shape_z[g] * charge[0:1, :]
        high = value.astype(BF16)
        rest = (value - high.astype(F32)).astype(BF16)
        total = total + dot_nt(shape_xy[g], high) + dot_nt(shape_xy[g], rest) + dot_nt(shape_low[g], high)
    den_ref[...] = total.reshape(SX, SY, GZ)

    for h in range(chunks):
        for o in range(OUT_CHUNKS):
            at = pl.ds(o * low, low)
            total = own_part[h, at, :]
            for k in range(1, nc):
                part_copy(k, h, o).wait_recv()
                total = total + part_in[k - 1, h, at, :].astype(F32)
            sq_ref[at, h * LANES : (h + 1) * LANES] = total.astype(BF16)

    for copy in w_copies:
        copy.wait_send()
    pack_copy.wait_send()
    for k in range(1, nr):
        v_copy(k).wait_send()
    for g, k in sent_q:
        q_copy(g, k).wait_send()
    for h in range(chunks):
        for k in range(1, nr // 2):
            piece_copy(k, h).wait_send()
        for i in range(ratio):
            for cc in range(nc):

                @pl.when(direct(i))
                def _():
                    fwd_copy(i, cc, h).wait_send()

    @pl.when(jnp.logical_not(at_home))
    def _():
        v_copy(0).wait_send()
        for h in range(chunks):
            piece_copy(0, h).wait_send()

    for k in range(1, nc):
        for h in range(chunks):
            for o in range(OUT_CHUNKS):
                part_copy(k, h, o).wait_send()


def store(sq_ref, den_ref, sq_out, den_out, sem):
    copies = [
        pltpu.make_async_copy(sq_ref, sq_out, sem.at[0]),
        pltpu.make_async_copy(den_ref, den_out, sem.at[1]),
    ]
    for copy in copies:
        copy.start()
    for copy in copies:
        copy.wait()


def local(sizes, density_matrix, block_mask, weights, exponents, anchor_x, anchor_y, anchor_z):
    nr, nc, nl = sizes
    ratio = nr // nc
    rows, cols = density_matrix.shape
    width = cols // nl
    dma = pltpu.SemaphoreType.DMA
    chunks = width // LANES
    pieces = ratio * nc * chunks
    outs = (nc - 1) * chunks * OUT_CHUNKS
    hbm = pl.BlockSpec(memory_space=pltpu.HBM)
    vmem = pl.BlockSpec(memory_space=pltpu.VMEM)
    inputs = (
        density_matrix, block_mask, weights.reshape(1, -1), exponents.reshape(1, -1),
        anchor_x, anchor_y, anchor_z,
    )
    shapes = (
        jax.ShapeDtypeStruct((rows, width), BF16),
        jax.ShapeDtypeStruct((SX, SY, GZ), F32),
    )
    results = pl.pallas_call(
        functools.partial(kernel, sizes),
        out_shape=(pltpu.VMEM((rows, width), BF16), pltpu.VMEM((SX, SY, GZ), F32)),
        in_specs=[hbm] * 7,
        out_specs=(vmem, vmem),
        scratch_shapes=[
            pltpu.VMEM((rows, cols), BF16),
            pltpu.VMEM(block_mask.shape, jnp.int32),
            pltpu.VMEM((1, width), F32),
            pltpu.VMEM((1, rows), F32),
            pltpu.SMEM(anchor_x.shape, jnp.int32),
            pltpu.SMEM(anchor_x.shape, jnp.int32),
            pltpu.SMEM(anchor_x.shape, jnp.int32),
            dma((6 + LOADS,)),
            pltpu.VMEM((rows, cols), BF16),
            pltpu.VMEM((ratio, nc, chunks, rows, LANES), BF16),
            pltpu.VMEM((chunks, rows, LANES), F32),
            pltpu.VMEM((nc - 1, chunks, rows, LANES), BF16),
            pltpu.VMEM((nc - 1, chunks, rows, LANES), BF16),
            pltpu.VMEM((nl, 8, width), F32),
            pltpu.VMEM((8, rows), F32),
            pltpu.VMEM((ratio, nc, 8, rows), F32),
            pltpu.VMEM((8, rows), F32),
            pltpu.VMEM((2, nc, 8, rows), F32),
            pltpu.VMEM((8, rows), F32),
            pltpu.VMEM((8, rows), F32),
            pltpu.VMEM((2, SX * SY, rows), BF16),
            pltpu.VMEM((2, SX * SY, rows), BF16),
            pltpu.VMEM((2, GZ, rows), F32),
            dma((nr // 2 * chunks,)),
            dma((pieces,)),
            dma((pieces,)),
            dma((outs,)),
            dma((outs,)),
            dma((nl - 1,)),
            dma((nl - 1,)),
            dma((nr,)),
            dma((ratio * nc,)),
            dma((2 * nc,)),
            dma((2 * nc,)),
            dma((1,)),
            dma((1,)),
        ],
        compiler_params=pltpu.CompilerParams(
            collective_id=0, has_side_effects=True, vmem_limit_bytes=66_000_000
        ),
        name="square_collocate",
    )(*[pltpu.with_memory_space_constraint(x, pltpu.HBM) for x in inputs])
    return pl.pallas_call(
        store,
        out_shape=shapes,
        in_specs=[vmem] * 2,
        out_specs=(hbm, hbm),
        scratch_shapes=[dma((2,))],
        compiler_params=pltpu.CompilerParams(vmem_limit_bytes=4 * 1024 * 1024),
        name="store",
    )(*results)


def solution(mesh):
    sizes = (mesh.shape["row"], mesh.shape["col"], mesh.shape["layer"])
    return jax.shard_map(
        functools.partial(local, sizes),
        mesh=mesh,
        in_specs=(
            P("row", "col"), P("row", "col"), P(("col", "layer")),
            P("row"), P("row"), P("row"), P("row"),
        ),
        out_specs=(P("row", ("col", "layer")), P("row", ("col", "layer"), None)),
        check_vma=False,
    )
```

profile of v0, /device:TPU:0, one launch (start us, length us, event | category | flops | bytes accessed | tf_op | source)
XLA Modules:
  0.0 22.4 jit_solution(1423581517980012625)
XLA Ops:
  0.6 21.0 %square_collocate.1 = (bf16[512,256]{1,0:T(8,128)(2,1)S(1)}, f32[32,16,128]{2,1,0:T(8,128)S(1)}) custom-call(bf16[512,1024]{1,0:T(8,128)(2,1)} %a_hbm.1, s32[8,16]{1,0:T(8,128)} %mask_hbm.1, f32[1,256]{1,0:T(1,128)} %bitcast.3, f32[1,512]{1,0:T(1,128)} %bitcast.2, s32[8]{0:T(128)} %ax_hbm.1, s32[8]{0:T(128)} %ay_hbm.1, s32[8]{0:T(128)} %az_hbm.1), custom_call_target="tpu_custom_call" | custom-call | tf_op jit(solution)/shard_map/square_collocate/pallas_call | solution.py:390
  21.6 0.8 %store.1 = (bf16[512,256]{1,0:T(8,128)(2,1)}, f32[32,16,128]{2,1,0:T(8,128)}) custom-call(bf16[512,256]{1,0:T(8,128)(2,1)S(1)} %get-tuple-element.4.sq_ref, f32[32,16,128]{2,1,0:T(8,128)S(1)} %get-tuple-element.5.den_ref), custom_call_target="tpu_custom_call" | custom-call | tf_op jit(solution)/shard_map/store/pallas_call | solution.py:438
where the time goes:
time: 22.6 us; the launch traced here: 22.4 us
  Pallas kernels  21.8 us (96%)
  between operations  0.64 us (3%)
    pallas_call x1, Pallas kernels, local(): pl.pallas_call(functools.partial(kernel, sizes), out_shape=(pltpu.VMEM((r...  21 us
    pallas_call x1, Pallas kernels, local(): pl.pallas_call(store, out_shape=shapes, in_specs=[vmem] * 2, out_specs=(h...  0.81 us

commit v1 on v0

v1 whole, which is shorter than its diff:
```python
import functools

import jax
import jax.numpy as jnp
from jax import lax
from jax.experimental import pallas as pl
from jax.experimental.pallas import tpu as pltpu
from jax.sharding import PartitionSpec as P

BLOCK = 64
TILE = 16
SX = 32
SY = 16
GZ = 128
STEP_SQ = 0.0625
MESH = pl.DeviceIdType.MESH
F32 = jnp.float32
BF16 = jnp.bfloat16
LANES = 128
OUT_CHUNKS = 2
LOADS = 2
SUB = 2
EARLY = 2
CHARGE_AT = 1
DETOUR = (1, 0, 0, 0)


def dot_nt(a, b):
    return lax.dot_general(a, b, (((1,), (1,)), ((), ())), preferred_element_type=F32)


def hi_lo(x):
    high = x.astype(BF16).astype(F32)
    return jnp.concatenate([high, x - high], axis=0).astype(BF16)


def kernel(
    sizes,
    a_hbm, mask_hbm, w_hbm, e_hbm, ax_hbm, ay_hbm, az_hbm,
    sq_ref, den_ref,
    a_ref, mask_ref, w_ref, e_ref, ax_ref, ay_ref, az_ref, load_sem,
    m_buf, mine, wide, right, own_part, part_out, part_in, detour,
    v_out, v_all, q_out, q_all, pack, pack_in, shape_xy, shape_low, shape_z,
    piece_send, piece_recv, fwd_send, relay_send, own_sem, part_send, part_recv, detour_recv, detour_send,
    v_send, v_recv, q_send, q_recv, pack_send, pack_recv, ready, below, above,
):
    nr, nc, nl = sizes
    ratio = nr // nc
    square = nr == 4 and nc == 2
    rows, cols = a_ref.shape
    width = cols // nl
    atoms = rows // BLOCK
    r, c, l = lax.axis_index("row"), lax.axis_index("col"), lax.axis_index("layer")
    sibling = r + 1 - 2 * (r % 2)
    following = (r + 1) % nr
    home = r // ratio
    slot = r % ratio
    at_home = home == c
    away = jnp.logical_not(at_home)
    across = (r + 2) % nr
    other = (c + 1) % nc

    def remote(src, dst, send, recv, device):
        return pltpu.make_async_remote_copy(
            src_ref=src, dst_ref=dst, send_sem=send, recv_sem=recv,
            device_id=device, device_id_type=MESH,
        )

    def signal(sem, device):
        pl.semaphore_signal(sem, inc=1, device_id=device, device_id_type=MESH)

    chunks = width // LANES
    tall = rows // LOADS
    part_rows = rows // SUB
    small = [
        pltpu.make_async_copy(src, dst, load_sem.at[at])
        for at, (src, dst) in enumerate((
            (mask_hbm, mask_ref), (w_hbm, w_ref), (e_hbm, e_ref),
            (ax_hbm, ax_ref), (ay_hbm, ay_ref), (az_hbm, az_ref),
        ))
    ]
    large = [
        pltpu.make_async_copy(
            a_hbm.at[pl.ds(p * tall, tall), :], a_ref.at[pl.ds(p * tall, tall), :], load_sem.at[6 + p]
        )
        for p in range(LOADS)
    ]

    barrier = pltpu.get_barrier_semaphore()
    if square:
        peers = [(dr, 0, 0) for dr in range(1, nr)]
        for dr in (0, 1):
            signal(barrier, ((r // 2) * 2 + (r + dr) % 2, other, l))
        n_peers = 2
    else:
        peers = [
            (dr, dc, dl) for dr in range(nr) for dc in range(nc) for dl in range(nl)
            if (dr or dc or dl) and (dl == 0 or dr in (0, 1, nr - 1))
        ]
        n_peers = 0
    for dr, dc, dl in peers:
        signal(barrier, ((r + dr) % nr, (c + dc) % nc, (l + dl) % nl))
    n_peers += len(peers)
    has_above = l + 1 < nl
    has_below = l > 0

    def to_layers(up, down):
        @pl.when(has_above)
        def _():
            signal(up, (r, c, l + 1))

        @pl.when(has_below)
        def _():
            signal(down, (r, c, l - 1))

    if square:
        to_layers(barrier, barrier)
    for copy in small + large:
        copy.start()

    for copy in small:
        copy.wait()
    kept = jnp.where(mask_ref[...] > 0, 1.0, 0.0).astype(F32)
    spread = lax.broadcasted_iota(jnp.int32, (cols // BLOCK, cols), 1) // BLOCK
    pick = lax.broadcasted_iota(jnp.int32, (cols // BLOCK, cols), 0)
    wide[...] = jnp.dot(kept, jnp.where(spread == pick, 1.0, 0.0).astype(F32), preferred_element_type=F32)
    strip = pl.ds(pl.multiple_of(l * width, LANES), width)
    for b in range(atoms):
        if b % (atoms // LOADS) == 0:
            large[b // (atoms // LOADS)].wait()
        at = pl.ds(b * BLOCK, BLOCK)
        mine[at, :] = a_ref[at, strip] * jnp.broadcast_to(wide[b : b + 1, strip], (BLOCK, width)).astype(BF16)

    def squash(total):
        return total[0:1, :] + total[8:9, :]

    v_out[...] = squash(dot_nt(hi_lo(jnp.broadcast_to(w_ref[...], (8, width))), mine[...]))

    if square:
        n_peers = n_peers + has_above.astype(jnp.int32) + has_below.astype(jnp.int32)
    pl.semaphore_wait(barrier, n_peers)
    if square:
        signal(ready.at[0], (across, c, l))

    def v_copy(k):
        return remote(
            v_out, v_all.at[slot, c], v_send.at[k], v_recv.at[slot * nc + c], ((r + k) % nr, home, l)
        )

    def mine_at(h, s):
        return mine.at[pl.ds(s * part_rows, part_rows), pl.ds(h * LANES, LANES)]

    def piece(i, cc, h, s):
        return right.at[i, cc, h, pl.ds(s * part_rows, part_rows), :]

    def sem_at(i, cc, h, s):
        return ((i * nc + cc) * chunks + h) * SUB + s

    def piece_copy(k, h, s):
        return remote(
            mine_at(h, s), piece(slot, c, h, s), piece_send.at[(k * chunks + h) * SUB + s],
            piece_recv.at[sem_at(slot, c, h, s)], ((r + 2 * k) % nr, home, l),
        )

    def own_copy(h, s):
        return pltpu.make_async_copy(mine_at(h, s), piece(slot, c, h, s), own_sem.at[h * SUB + s])

    def own_fwd(h, s):
        return remote(
            mine_at(h, s), piece(slot, c, h, s), fwd_send.at[sem_at(slot, c, h, s)],
            piece_recv.at[sem_at(slot, c, h, s)], (sibling, c, l),
        )

    def fwd_copy(i, cc, h, s):
        return remote(
            piece(i, cc, h, s), piece(i, cc, h, s), fwd_send.at[sem_at(i, cc, h, s)],
            piece_recv.at[sem_at(i, cc, h, s)], (sibling, c, l),
        )

    def relay_copy(h, s):
        return remote(
            piece(slot, other, h, s), piece(slot, other, h, s), relay_send.at[h * SUB + s],
            piece_recv.at[sem_at(slot, other, h, s)], (across, c, l),
        )

    def landed(i, cc, h, s):
        fwd_copy(i, cc, h, s).wait_recv()

    units = [(h, s) for h in range(chunks) for s in range(SUB)]
    relayed = [u for u in units if square and u[0] == chunks - 1]
    straight = [u for u in units if u not in relayed]
    order = relayed + straight

    @pl.when(at_home)
    def _():
        v_all[slot, c] = v_out[...]
        for k in range(1, nr):
            v_copy(k).start()
        for h, s in units:
            own_copy(h, s).start()
        for h, s in units:
            own_fwd(h, s).start()
        if not square:
            for h, s in units:
                for k in range(1, nr // 2):
                    piece_copy(k, h, s).start()
        else:
            for h, s in order[:EARLY]:
                piece_copy(1, h, s).start()

    if square:
        near = (r // 2) * 2

        @pl.when(away)
        def _():
            v_copy(0).start()

            @pl.when(slot == 0)
            def _():
                v_copy(1).start()

            @pl.when(slot == 1)
            def _():
                v_copy(3).start()

            for h, s in order:
                piece_copy(0, h, s).start()
    else:
        @pl.when(away)
        def _():
            for k in range(nr):
                v_copy(k).start()
            for h, s in units:
                for k in range(nr // 2):
                    piece_copy(k, h, s).start()

    lane_atom = lax.broadcasted_iota(jnp.int32, (8, rows), 1) // BLOCK
    sub = lax.broadcasted_iota(jnp.int32, (8, rows), 0)
    table = jnp.broadcast_to(e_ref[...], (8, rows))
    for j in range(atoms):
        here = lane_atom == j
        for at, ref in ((1, ax_ref), (2, ay_ref), (3, az_ref)):
            table = jnp.where(here & (sub == at), ref[j].astype(F32), table)
    pack[...] = table
    pack_copy = remote(pack, pack_in, pack_send.at[0], pack_recv.at[0], (following, c, l))
    pack_copy.start()

    for b in range(atoms):
        at = pl.ds(b * BLOCK, BLOCK)
        m_buf[at, :] = a_ref[at, :] * jnp.broadcast_to(wide[b : b + 1, :], (BLOCK, cols)).astype(BF16)

    if square:
        pl.semaphore_wait(ready.at[0], 1)

        @pl.when(away)
        def _():
            v_copy(2).start()

            @pl.when(slot == 0)
            def _():
                v_copy(3).start()

            @pl.when(slot == 1)
            def _():
                v_copy(1).start()

            for h, s in straight:
                piece_copy(1, h, s).start()

        to_layers(below.at[0], above.at[0])

    def layer_step(at):
        @pl.when(has_above)
        def _():
            pl.semaphore_wait(above.at[at], 1)

        @pl.when(has_below)
        def _():
            pl.semaphore_wait(below.at[at], 1)

        if at + 1 < nl - 1:
            to_layers(below.at[at + 1], above.at[at + 1])

    y_first = (c * nl + l) * SY
    y_count = nc * nl * SY

    def profiles(g, ref):
        rate = ref[0:1, :] * (-STEP_SQ)

        def profile(t):
            value = jnp.exp(rate * (t - 7.5) * (t - 7.5))
            return jnp.where((t >= 0.0) & (t < float(TILE)), value, 0.0)

        tx = lax.broadcasted_iota(jnp.int32, (SX, rows), 0).astype(F32) + float(g * SX) - ref[1:2, :]
        ty = (lax.broadcasted_iota(jnp.int32, (SY, rows), 0) + y_first).astype(F32) - ref[2:3, :]
        ty = jnp.where(ty < 0.0, ty + float(y_count), ty)
        tz = lax.broadcasted_iota(jnp.int32, (GZ, rows), 0).astype(F32) - ref[3:4, :]
        tz = jnp.where(tz < 0.0, tz + float(GZ), tz)
        px, py = profile(tx), profile(ty)
        for x in range(SX):
            plane = px[x : x + 1, :] * py
            high = plane.astype(BF16)
            shape_xy[g, x * SY : (x + 1) * SY, :] = high
            shape_low[g, x * SY : (x + 1) * SY, :] = (plane - high.astype(F32)).astype(BF16)
        shape_z[g] = profile(tz)

    profiles(0, pack)
    if square:
        layer_step(0)

    def direct(i):
        return (c * ratio + i) % 2 == r % 2

    def pass_on(h, s, ks):
        for k in ks:
            cc = (c + k) % nc
            for i in range(ratio):

                @pl.when(direct(i) & jnp.logical_not((c * ratio + i == r) & (cc == c)))
                def _():
                    landed(i, cc, h, s)
                    fwd_copy(i, cc, h, s).start()

    def turn(j):
        if not square:
            return j
        return jnp.where(at_home, (j + 1) % chunks, j)

    def take(cc, h):
        for s in range(SUB):
            for i in range(ratio):

                @pl.when(jnp.logical_not(direct(i)))
                def _():
                    landed(i, cc, h, s)

    low = rows // OUT_CHUNKS

    def product(cc, h, at):
        total = jnp.dot(m_buf[at, 0:rows], right[0, cc, h], preferred_element_type=F32)
        for i in range(1, ratio):
            total = total + jnp.dot(
                m_buf[at, i * rows : (i + 1) * rows], right[i, cc, h], preferred_element_type=F32
            )
        return total

    outs = [(h, o) for h in range(chunks) for o in range(OUT_CHUNKS)]
    bent = [u for u in outs if square and DETOUR[u[0] * OUT_CHUNKS + u[1]]]

    def part_index(k, h, o):
        return ((k - 1) * chunks + h) * OUT_CHUNKS + o

    def part_copy(k, h, o):
        at = pl.ds(o * low, low)
        index = part_index(k, h, o)
        return remote(
            part_out.at[k - 1, h, at, :], part_in.at[k - 1, h, at, :], part_send.at[index],
            part_recv.at[index], (r, (c + k) % nc, l),
        )

    def bend_copy(h, o):
        at = pl.ds(o * low, low)
        return remote(
            part_out.at[0, h, at, :], detour.at[bent.index((h, o))], part_send.at[part_index(1, h, o)],
            detour_recv.at[bent.index((h, o))], (across, other, l),
        )

    def unbend_copy(h, o):
        at = pl.ds(o * low, low)
        return remote(
            detour.at[bent.index((h, o))], part_in.at[0, h, at, :], detour_send.at[bent.index((h, o))],
            part_recv.at[part_index(1, h, o)], (across, c, l),
        )

    def parts(j):
        h = turn(j)
        for k in range(1, nc):
            take((c + k) % nc, h)
            for o in range(OUT_CHUNKS):
                at = pl.ds(o * low, low)
                part_out[k - 1, h, at, :] = product((c + k) % nc, h, at).astype(BF16)
                if (j, o) in bent:

                    @pl.when(at_home)
                    def _():
                        part_copy(k, h, o).start()

                    @pl.when(away)
                    def _():
                        bend_copy(j, o).start()

                else:
                    part_copy(k, h, o).start()

    def unbend():
        @pl.when(away)
        def _():
            for h, o in bent:
                bend_copy(h, o).wait_recv()
                unbend_copy(h, o).start()

    def charge_share():
        for i in range(ratio):
            for cc in range(nc):

                @pl.when(jnp.logical_not((c * ratio + i == r) & (cc == c)))
                def _():
                    remote(
                        v_out, v_all.at[i, cc], v_send.at[0], v_recv.at[i * nc + cc], (sibling, c, l)
                    ).wait_recv()

        total = jnp.zeros((16, rows), F32)
        for i in range(ratio):
            v = v_all[i, 0]
            for cc in range(1, nc):
                v = v + v_all[i, cc]
            total = total + dot_nt(hi_lo(jnp.broadcast_to(v, (8, rows))), m_buf[:, i * rows : (i + 1) * rows])
        q_out[...] = squash(total)
        q_all[0, c, l] = q_out[...]

    def q_copy(g, k, m):
        index = (g * nc + k) * nl + m
        return remote(
            q_out, q_all.at[g, c, l], q_send.at[index], q_recv.at[index],
            ((r + g) % nr, (c + k) % nc, (l + m) % nl),
        )

    sent_q = [(g, k, m) for m in reversed(range(nl)) for g in range(2) for k in range(nc) if g or k or m]

    def own_late():
        if square:

            @pl.when(at_home)
            def _():
                for h, s in order[EARLY:]:
                    piece_copy(1, h, s).start()

    def charges():
        if square:
            layer_step(1)
        charge_share()
        if square:
            for at in range(2, nl - 1):
                layer_step(at)
        for g, k, m in sent_q:
            q_copy(g, k, m).start()

    if CHARGE_AT == 0:
        charges()
    for j in range(chunks):
        for s in range(SUB):
            pass_on(turn(j), s, range(1, nc))
            if square and j == 0:

                @pl.when(at_home)
                def _():
                    relay_copy(turn(j), s).start()

        if j == 0:
            own_late()
            if CHARGE_AT == 1:
                charges()
        parts(j)
        if j == 0:
            if CHARGE_AT == 2:
                charges()
            pack_copy.wait_recv()
            profiles(1, pack_in)
    unbend()
    for h, s in units:
        pass_on(h, s, (0,))

    @pl.when(at_home)
    def _():
        for h, s in units:
            own_copy(h, s).wait()

    for h in range(chunks):
        take(c, h)
        for o in range(OUT_CHUNKS):
            at = pl.ds(o * low, low)
            own_part[h, at, :] = product(c, h, at)

    for g, k, m in sent_q:
        q_copy(g, k, m).wait_recv()
    total = jnp.zeros((SX * SY, GZ), F32)
    for g in range(2):
        charge = jnp.zeros((1, rows), F32)
        for cc in range(nc):
            for ll in range(nl):
                charge = charge + q_all[g, cc, ll]
        value = shape_z[g] * charge
        high = value.astype(BF16)
        rest = (value - high.astype(F32)).astype(BF16)
        total = total + dot_nt(shape_xy[g], high) + dot_nt(shape_xy[g], rest) + dot_nt(shape_low[g], high)
    den_ref[...] = total.reshape(SX, SY, GZ)

    for h in range(chunks):
        for o in range(OUT_CHUNKS):
            at = pl.ds(o * low, low)
            total = own_part[h, at, :]
            for k in range(1, nc):
                part_copy(k, h, o).wait_recv()
                total = total + part_in[k - 1, h, at, :].astype(F32)
            sq_ref[at, h * LANES : (h + 1) * LANES] = total.astype(BF16)

    pack_copy.wait_send()
    for g, k, m in sent_q:
        q_copy(g, k, m).wait_send()
    for k in range(1, nr):
        v_copy(k).wait_send()
    for i in range(ratio):
        for cc in range(nc):

            @pl.when(direct(i))
            def _():
                for h, s in units:
                    fwd_copy(i, cc, h, s).wait_send()

    @pl.when(at_home)
    def _():
        for k in range(1, nr // 2):
            for h, s in units:
                piece_copy(k, h, s).wait_send()
        for h, s in relayed:
            relay_copy(h, s).wait_send()

    @pl.when(away)
    def _():
        v_copy(0).wait_send()
        for h, s in units:
            piece_copy(0, h, s).wait_send()
        for k in range(1, nr // 2):
            for h, s in straight:
                piece_copy(k, h, s).wait_send()
        for h, o in bent:
            unbend_copy(h, o).wait_send()

    for k in range(1, nc):
        for h, o in outs:
            part_copy(k, h, o).wait_send()


def store(sq_ref, den_ref, sq_out, den_out, sem):
    copies = [
        pltpu.make_async_copy(sq_ref, sq_out, sem.at[0]),
        pltpu.make_async_copy(den_ref, den_out, sem.at[1]),
    ]
    for copy in copies:
        copy.start()
    for copy in copies:
        copy.wait()


def local(sizes, density_matrix, block_mask, weights, exponents, anchor_x, anchor_y, anchor_z):
    nr, nc, nl = sizes
    ratio = nr // nc
    rows, cols = density_matrix.shape
    width = cols // nl
    dma = pltpu.SemaphoreType.DMA
    chunks = width // LANES
    pieces = ratio * nc * chunks
    outs = (nc - 1) * chunks * OUT_CHUNKS
    hbm = pl.BlockSpec(memory_space=pltpu.HBM)
    vmem = pl.BlockSpec(memory_space=pltpu.VMEM)
    inputs = (
        density_matrix, block_mask, weights.reshape(1, -1), exponents.reshape(1, -1),
        anchor_x, anchor_y, anchor_z,
    )
    shapes = (
        jax.ShapeDtypeStruct((rows, width), BF16),
        jax.ShapeDtypeStruct((SX, SY, GZ), F32),
    )
    results = pl.pallas_call(
        functools.partial(kernel, sizes),
        out_shape=(pltpu.VMEM((rows, width), BF16), pltpu.VMEM((SX, SY, GZ), F32)),
        in_specs=[hbm] * 7,
        out_specs=(vmem, vmem),
        scratch_shapes=[
            pltpu.VMEM((rows, cols), BF16),
            pltpu.VMEM(block_mask.shape, jnp.int32),
            pltpu.VMEM((1, width), F32),
            pltpu.VMEM((1, rows), F32),
            pltpu.SMEM(anchor_x.shape, jnp.int32),
            pltpu.SMEM(anchor_x.shape, jnp.int32),
            pltpu.SMEM(anchor_x.shape, jnp.int32),
            dma((6 + LOADS,)),
            pltpu.VMEM((rows, cols), BF16),
            pltpu.VMEM((rows, width), BF16),
            pltpu.VMEM((rows // BLOCK, cols), F32),
            pltpu.VMEM((ratio, nc, chunks, rows, LANES), BF16),
            pltpu.VMEM((chunks, rows, LANES), F32),
            pltpu.VMEM((nc - 1, chunks, rows, LANES), BF16),
            pltpu.VMEM((nc - 1, chunks, rows, LANES), BF16),
            pltpu.VMEM((len(DETOUR), rows // OUT_CHUNKS, LANES), BF16),
            pltpu.VMEM((1, rows), F32),
            pltpu.VMEM((ratio, nc, 1, rows), F32),
            pltpu.VMEM((1, rows), F32),
            pltpu.VMEM((2, nc, nl, 1, rows), F32),
            pltpu.VMEM((8, rows), F32),
            pltpu.VMEM((8, rows), F32),
            pltpu.VMEM((2, SX * SY, rows), BF16),
            pltpu.VMEM((2, SX * SY, rows), BF16),
            pltpu.VMEM((2, GZ, rows), F32),
            dma((nr // 2 * chunks * SUB,)),
            dma((pieces * SUB,)),
            dma((pieces * SUB,)),
            dma((chunks * SUB,)),
            dma((chunks * SUB,)),
            dma((outs,)),
            dma((outs,)),
            dma((len(DETOUR),)),
            dma((len(DETOUR),)),
            dma((nr,)),
            dma((ratio * nc,)),
            dma((2 * nc * nl,)),
            dma((2 * nc * nl,)),
            dma((1,)),
            dma((1,)),
            pltpu.SemaphoreType.REGULAR((1,)),
            pltpu.SemaphoreType.REGULAR((max(nl - 1, 1),)),
            pltpu.SemaphoreType.REGULAR((max(nl - 1, 1),)),
        ],
        compiler_params=pltpu.CompilerParams(
            collective_id=0, has_side_effects=True, vmem_limit_bytes=66_000_000
        ),
        name="square_collocate",
    )(*[pltpu.with_memory_space_constraint(x, pltpu.HBM) for x in inputs])
    return pl.pallas_call(
        store,
        out_shape=shapes,
        in_specs=[vmem] * 2,
        out_specs=(hbm, hbm),
        scratch_shapes=[dma((2,))],
        compiler_params=pltpu.CompilerParams(vmem_limit_bytes=4 * 1024 * 1024),
        name="store",
    )(*results)


def solution(mesh):
    sizes = (mesh.shape["row"], mesh.shape["col"], mesh.shape["layer"])
    return jax.shard_map(
        functools.partial(local, sizes),
        mesh=mesh,
        in_specs=(
            P("row", "col"), P("row", "col"), P(("col", "layer")),
            P("row"), P("row"), P("row"), P("row"),
        ),
        out_specs=(P("row", ("col", "layer")), P("row", ("col", "layer"), None)),
        check_vma=False,
    )
```

time: 22.6 us -> 21.1 us (0.934)
  Pallas kernels: 21.8 us -> 20.3 us
    pallas_call x1, Pallas kernels: 21 us -> 19.4 us  [local(): pl.pallas_call(functools.partial(kernel, sizes), out_shape=(pltpu.VMEM((r...]
where the time goes in v1:
time: 21.1 us; the launch traced here: 20.9 us
  Pallas kernels  20.3 us (96%)
  between operations  0.64 us (3%)
    pallas_call x1, Pallas kernels, local(): pl.pallas_call(functools.partial(kernel, sizes), out_shape=(pltpu.VMEM((r...  19.4 us
    pallas_call x1, Pallas kernels, local(): pl.pallas_call(store, out_shape=shapes, in_specs=[vmem] * 2, out_specs=(h...  0.81 us

profile of v1, /device:TPU:0, one launch (start us, length us, event | category | flops | bytes accessed | tf_op | source)
XLA Modules:
  0.0 20.9 jit_solution(4156602790356782671)
XLA Ops:
  0.6 19.4 %square_collocate.1 = (bf16[512,256]{1,0:T(8,128)(2,1)S(1)}, f32[32,16,128]{2,1,0:T(8,128)S(1)}) custom-call(bf16[512,1024]{1,0:T(8,128)(2,1)} %a_hbm.1, s32[8,16]{1,0:T(8,128)} %mask_hbm.1, f32[1,256]{1,0:T(1,128)} %bitcast.3, f32[1,512]{1,0:T(1,128)} %bitcast.2, s32[8]{0:T(128)} %ax_hbm.1, s32[8]{0:T(128)} %ay_hbm.1, s32[8]{0:T(128)} %az_hbm.1), custom_call_target="tpu_custom_call" | custom-call | tf_op jit(solution)/shard_map/square_collocate/pallas_call | solution.py:574
  20.1 0.8 %store.1 = (bf16[512,256]{1,0:T(8,128)(2,1)}, f32[32,16,128]{2,1,0:T(8,128)}) custom-call(bf16[512,256]{1,0:T(8,128)(2,1)S(1)} %get-tuple-element.4.sq_ref, f32[32,16,128]{2,1,0:T(8,128)S(1)} %get-tuple-element.5.den_ref), custom_call_target="tpu_custom_call" | custom-call | tf_op jit(solution)/shard_map/store/pallas_call | solution.py:629
